TPU v7x, 32 devices: a whole 2x2x4 slice. The times are simulated.
32 devices in a mesh: grp: 2 (over x), row: 16 (over z, y, core).
Axes of the slice: x: 2, y: 2, z: 4, core: 2. Of those that a mesh axis runs over, the one named last changes fastest.
Arguments:
- greens: bfloat16 [8192, 16384], P(('grp', 'row')), parts along dimension 0, may hold values from -0.0625 to 0.0625
- track_id: int32 [8192], P(('grp', 'row')), parts along dimension 0, may hold values from 0 to 7
- sigma_inv: float32 [16], P('grp'), parts along dimension 0, may hold values from 1 to 10
- sketch: float32 [192, 128, 128], P('grp', 'row'), parts along dimension 0, may hold values from -6 to 6
Outputs:
- range_basis: float32 [8192, 96], P(('grp', 'row')), parts along dimension 0
- coefficients: float32 [256, 128, 96], P(('grp', 'row')), parts along dimension 0
There are 2 independent parts, one for each index of `grp`. A program takes and returns all parts, laid end to end along the dimension named above; each array names one. Nothing has to cross between parts.
All inputs are finite; a program needn't handle non-finite values.
Results may differ from a plain program's by a relative error of at most 0.011.
Values may be sent and summed in bfloat16 or wider, within the bound.
No kernel may reach another device: no remote copies, remote signals or barrier semaphores. Data moves between devices by JAX's collectives and lax.ppermute only.
A program may use at most 128 MiB of HBM per device.

v0:
```python
import jax
import jax.numpy as jnp
from jax import lax
from jax.sharding import PartitionSpec as P

SWEEPS = 4
smoothing = 0.24


def with_halo(x, sides, width):
    for axis, dim in sides:
        count, length = (lax.axis_size(axis), x.shape[dim])
        up = [(i, (i + 1) % count) for i in range(count - 1)]
        down = [(j, i) for i, j in up]
        last = lax.slice_in_dim(x, length - width, length, axis=dim)
        initial = lax.slice_in_dim(x, 0, width, axis=dim)
        before = lax.ppermute(last, axis, up)
        after = lax.ppermute(initial, axis, down)
        x = jnp.concatenate([before, x, after], axis=dim)
    return x


def smooth_padded(padded, field):
    padded = jnp.pad(padded, ((0, 0), (0, 0), (1, 1)))
    beside_all = (
        padded[:, 2:, 1:-1] + padded[:, :-2, 1:-1] + padded[:, 1:-1, 2:] + padded[:, 1:-1, :-2]
    )
    return field + smoothing * (beside_all - 4.0 * field)


def orthonormalize(sketched, total_rows):
    local_gram = jnp.dot(sketched.T, sketched, precision=lax.Precision.HIGHEST)
    gram_matrix = lax.psum(local_gram, "row") / total_rows
    factor = jnp.linalg.cholesky(gram_matrix)
    return lax.linalg.triangular_solve(
        factor, sketched, left_side=False, lower=True, transpose_a=True
    )


def local(greens, track_id, sigma_inv, sketch):
    local_rows = greens.shape[0]
    columns_count = sketch.shape[0]
    total_rows = local_rows * lax.axis_size("row")
    row_scale = 1.0 / jnp.sqrt(jnp.float32(total_rows))
    groups = jnp.arange(sigma_inv.shape[0], dtype=jnp.int32)
    onehot = (track_id[:, None] == groups[None, :]).astype(jnp.float32)
    weights = jnp.dot(onehot, sigma_inv, precision=lax.Precision.HIGHEST)
    field = sketch
    for sweep_index in range(SWEEPS):
        padded = with_halo(field, (("row", 1),), 1)
        field = smooth_padded(padded, field)
    omega = field.astype(jnp.bfloat16)
    portion = lax.all_gather(omega, "row", axis=1, tiled=True)
    strike = portion.shape[2]
    width = portion.shape[1] * strike
    columns = greens
    flattened = portion.reshape(portion.shape[0], width)
    first = lax.dot_general(
        columns, flattened, (((1,), (1,)), ((), ())), preferred_element_type=jnp.float32
    )
    basis_one = orthonormalize(first * weights[:, None], total_rows)
    weighted_one = (basis_one * weights[:, None]).astype(jnp.bfloat16)
    columns = greens
    back_local = lax.psum_scatter(
        lax.dot_general(
            columns, weighted_one, (((0,), (0,)), ((), ())), preferred_element_type=jnp.float32
        ),
        "row",
        scatter_dimension=0,
        tiled=True,
    )
    back_local = (back_local * row_scale).astype(jnp.bfloat16)
    columns = greens
    second = jnp.dot(
        columns,
        lax.all_gather(back_local, "row", axis=0, tiled=True),
        preferred_element_type=jnp.float32,
    )
    range_basis = orthonormalize(second * weights[:, None], total_rows)
    weighted_two = (range_basis * weights[:, None]).astype(jnp.bfloat16)
    columns = greens
    projected = lax.psum_scatter(
        lax.dot_general(
            columns, weighted_two, (((0,), (0,)), ((), ())), preferred_element_type=jnp.float32
        ),
        "row",
        scatter_dimension=0,
        tiled=True,
    )
    coefficients = (projected * row_scale).reshape(sketch.shape[1], sketch.shape[2], columns_count)
    return (range_basis, coefficients)


def solution(mesh):
    in_specs = (P(("grp", "row"), None), P(("grp", "row")), P("grp"), P("grp", "row", None))
    out_specs = (P(("grp", "row"), None), P(("grp", "row"), None, None))
    return jax.shard_map(local, mesh=mesh, in_specs=in_specs, out_specs=out_specs, check_vma=False)
```

profile of v0, /device:TPU:0, one launch (start us, length us, event | category | flops | bytes accessed | tf_op | source)
XLA Modules:
  0.0 502.3 jit_solution(15993353237637454936)
XLA Ops:
  7.2 0.0 copy-start
  7.2 0.0 copy-start.1
  7.2 0.0 all-gather.3.cloned.1.call-start
  7.2 1.2 fusion.43
  8.5 2.4 collective-permute-start.1
  10.9 1.3 collective-permute-start
  12.2 3.9 collective-permute-done
  16.1 1.9 select_maximum_fusion.6
  18.0 0.3 fusion.24
  18.3 0.1 fusion.42
  18.4 4.7 collective-permute-start.3
  23.1 1.3 collective-permute-start.2
  24.4 0.0 collective-permute-done.3
  24.4 1.8 collective-permute-done.2
  26.2 0.9 select_maximum_fusion.4
  27.1 0.3 fusion.20
  27.4 0.1 fusion.41
  27.5 5.0 collective-permute-start.5
  32.5 1.3 collective-permute-start.4
  33.8 1.8 collective-permute-done.4
  35.6 0.9 select_maximum_fusion.2
  36.5 0.3 fusion.16
  36.8 0.1 fusion.40
  36.9 5.1 %collective-permute-start.7 = (f32[96,1,128]{2,1,0:T(1,128)S(1)}, f32[96,1,128]{2,1,0:T(1,128)S(1)}, u32[]{:S(2)}, u32[]{:S(2)}) collective-permute-start(f32[96,1,128]{2,1,0:T(1,128)S(1)} %get-tuple-element.6), channel_id=1, source_target_pairs={{0,1},{1,2},{2,3},{3,4},{4,5},{5,6},{6,7},{7,8},{8,9},{9,10},{10,1... | collective-permute-start | bytes 147464 | tf_op jit(solution)/shard_map/ppermute | solution.py:17
  42.0 0.0 copy-start.3
  42.0 1.3 collective-permute-start.6
  43.3 1.8 collective-permute-done.6
  45.2 0.9 select_maximum_fusion
  46.1 1.0 fusion.12
  47.1 0.0 all-gather.3.cloned.1.call-update
  47.1 0.0 reduce-scatter.3.cloned.1.call-start
  47.2 0.2 fusion.26
  47.3 50.3 %all-gather.3.cloned.1.call-done = bf16[96,128,128]{2,1,0:T(8,128)(2,1)} async-done(((bf16[96,8,128]{2,1,0:T(8,128)(2,1)}), bf16[96,128,128]{2,1,0:T(8,128)(2,1)}) %all-gather.3.cloned.1.call-update) | async-done | bytes 3145744 | tf_op jit(solution)/shard_map/all_gather | solution.py:53
  97.6 7.7 %fusion.5 = f32[96,256]{1,0:T(8,128)S(1)} fusion(bf16[256,16384]{1,0:T(8,128)(2,1)} %param.7, bf16[12,8,128,128]{3,2,1,0:T(8,128)(2,1)} %bitcast.61, f32[256]{0:T(256)S(1)} %bitcast.62), kind=kOutput, calls=%fused_computation.20 | convolution fusion | flops 805330944 | bytes 11633664 | tf_op jit(solution)/shard_map/dot_general | solution.py:58
  105.4 0.2 fusion.44
  105.6 58.9 %psum.14 = f32[96,96]{0,1:T(8,128)S(1)} all-reduce(f32[96,96]{0,1:T(8,128)S(1)} %fusion.44), channel_id=1, replica_groups=mesh['grp'=2,'row'=16] {'row'}, use_global_device_ids=true, to_apply=%region_0.1 | all-reduce | flops 9216 | bytes 73728 | tf_op jit(solution)/shard_map/psum | solution.py:33
  164.5 0.1 copy.7
  164.6 8.8 %cholesky.44 = f32[96,96]{1,0:T(8,128)S(1)} custom-call(f32[96,96]{1,0:T(8,128)S(1)} %fusion.35), custom_call_target="Cholesky" | custom-call | tf_op jit(solution)/shard_map/jit(cholesky)/cholesky | solution.py:34
  173.4 0.6 compare_reduce_fusion.1
  174.1 0.7 fusion.30
  174.7 7.4 %custom-call.6 = f32[1,96,96]{1,2,0:T(8,128)S(1)} custom-call(f32[1,96,96]{2,1,0:T(8,128)S(1)} %fusion.30), custom_call_target="InvertDiagBlocksLowerTriangular" | custom-call | tf_op jit(solution)/shard_map/triangular_solve/custom-call.0 | solution.py:35
  182.1 0.3 fusion.8
  182.4 7.5 %convolution_bitcast_fusion.1 = f32[16384,96]{0,1:T(8,128)} fusion(bf16[256,96]{0,1:T(8,128)(2,1)S(1)} %fusion.8, bf16[256,16384]{1,0:T(8,128)(2,1)} %param.7), kind=kOutput, calls=%fused_computation.1 | convolution fusion | flops 805306368 | bytes 14729216 | tf_op jit(solution)/shard_map/dot_general | solution.py:65
  189.9 0.0 reduce-scatter.3.cloned.1.call-update
  189.9 0.0 all-gather.5.cloned.1.call-start
  190.0 82.4 %reduce-scatter.3.cloned.1.call-done = f32[1024,96]{0,1:T(8,128)} async-done(((f32[16384,96]{0,1:T(8,128)}), f32[1024,96]{0,1:T(8,128)}) %reduce-scatter.3.cloned.1.call-update) | async-done | bytes 393232 | tf_op jit(solution)/shard_map/reduce_scatter | solution.py:64
  272.3 1.7 multiply_convert_fusion
  274.0 0.0 all-gather.5.cloned.1.call-update
  274.1 0.0 reduce-scatter.5.cloned.1.call-start
  274.1 45.6 %all-gather.5.cloned.1.call-done = bf16[16384,96]{0,1:T(8,128)(2,1)} async-done(((bf16[1024,96]{0,1:T(8,128)(2,1)}), bf16[16384,96]{0,1:T(8,128)(2,1)}) %all-gather.5.cloned.1.call-update) | async-done | bytes 3145744 | tf_op jit(solution)/shard_map/all_gather | solution.py:76
  319.7 7.1 %convolution_multiply_fusion = f32[96,256]{1,0:T(8,128)S(1)} fusion(bf16[16384,96]{0,1:T(8,128)(2,1)} %all-gather.5.cloned.1.call-done, bf16[256,16384]{1,0:T(8,128)(2,1)} %param.7, f32[256]{0:T(256)S(1)} %bitcast.64), kind=kOutput, calls=%fused_computation.17 | convolution fusion | flops 805330944 | bytes 11633664 | tf_op jit(solution)/shard_map/dot_general | solution.py:74
  326.8 0.2 fusion.45
  327.0 59.1 %psum.15 = f32[96,96]{0,1:T(8,128)S(1)} all-reduce(f32[96,96]{0,1:T(8,128)S(1)} %fusion.45), channel_id=1, replica_groups=mesh['grp'=2,'row'=16] {'row'}, use_global_device_ids=true, to_apply=%region_4.7 | all-reduce | flops 9216 | bytes 73728 | tf_op jit(solution)/shard_map/psum | solution.py:33
  386.2 0.1 copy.9
  386.3 8.8 %cholesky.55 = f32[96,96]{1,0:T(8,128)S(1)} custom-call(f32[96,96]{1,0:T(8,128)S(1)} %fusion.33), custom_call_target="Cholesky" | custom-call | tf_op jit(solution)/shard_map/jit(cholesky)/cholesky | solution.py:34
  395.1 0.6 compare_reduce_fusion
  395.7 0.7 fusion.31
  396.4 7.4 %custom-call.7 = f32[1,96,96]{1,2,0:T(8,128)S(1)} custom-call(f32[1,96,96]{2,1,0:T(8,128)S(1)} %fusion.31), custom_call_target="InvertDiagBlocksLowerTriangular" | custom-call | tf_op jit(solution)/shard_map/triangular_solve/custom-call.0 | solution.py:35
  403.7 0.3 convolution_bitcast_fusion.2
  404.0 0.0 copy-start.2
  404.0 7.5 %convolution_bitcast_fusion = f32[16384,96]{0,1:T(8,128)} fusion(bf16[256,16384]{1,0:T(8,128)(2,1)} %param.7, f32[256,96]{0,1:T(8,128)S(1)} %convolution_bitcast_fusion.2, f32[256]{0:T(256)S(1)} %bitcast.65), kind=kOutput, calls=%fused_computation | convolution fusion | flops 805355520 | bytes 14779392 | tf_op jit(solution)/shard_map/dot_general | solution.py:83
  411.6 0.0 reduce-scatter.5.cloned.1.call-update
  411.6 82.4 %reduce-scatter.5.cloned.1.call-done = f32[1024,96]{0,1:T(8,128)} async-done(((f32[16384,96]{0,1:T(8,128)}), f32[1024,96]{0,1:T(8,128)}) %reduce-scatter.5.cloned.1.call-update) | async-done | bytes 393232 | tf_op jit(solution)/shard_map/reduce_scatter | solution.py:82
  494.0 1.8 copy_bitcast_fusion
  (13 shorter events, 0.1 us)
Async XLA Ops:
  7.2 40.0 %copy-start = (f32[8]{0:T(128)S(1)}, f32[8]{0:T(128)}, u32[]{:S(2)}) copy-start(f32[8]{0:T(128)} %param.9) | copy-start | bytes 100
  7.2 10.8 %copy-start.1 = (f32[96,8,128]{2,1,0:T(8,128)S(1)}, f32[96,8,128]{2,1,0:T(8,128)}, u32[]{:S(2)}) copy-start(f32[96,8,128]{2,1,0:T(8,128)} %param.10) | copy-start | bytes 1179652
  7.2 90.5 %all-gather.3.cloned.1.call-start = ((), (), s32[]{:S(2)}) async-start(), calls=%async_computation.2 | async-start | bytes 3342336 | tf_op jit(solution)/shard_map/all_gather | solution.py:53
  8.5 3.7 collective-permute-start.1
  10.9 5.2 %collective-permute-start = (f32[96,1,128]{2,1,0:T(1,128)S(1)}, f32[96,1,128]{2,1,0:T(1,128)S(1)}, u32[]{:S(2)}, u32[]{:S(2)}) collective-permute-start(f32[96,1,128]{2,1,0:T(1,128)S(1)} %get-tuple-element.13), channel_id=1, source_target_pairs={{1,0},{2,1},{3,2},{4,3},{5,4},{6,5},{7,6},{8,7},{9,8},{10,9},{11,1... | collective-permute-start | bytes 147464 | tf_op jit(solution)/shard_map/ppermute | solution.py:18
  18.4 6.0 %collective-permute-start.3 = (f32[96,1,128]{2,1,0:T(1,128)S(1)}, f32[96,1,128]{2,1,0:T(1,128)S(1)}, u32[]{:S(2)}, u32[]{:S(2)}) collective-permute-start(f32[96,1,128]{2,1,0:T(1,128)S(1)} %get-tuple-element.10), channel_id=1, source_target_pairs={{0,1},{1,2},{2,3},{3,4},{4,5},{5,6},{6,7},{7,8},{8,9},{9,10},{10,1... | collective-permute-start | bytes 147464 | tf_op jit(solution)/shard_map/ppermute | solution.py:17
  23.1 3.1 collective-permute-start.2
  27.5 6.3 %collective-permute-start.5 = (f32[96,1,128]{2,1,0:T(1,128)S(1)}, f32[96,1,128]{2,1,0:T(1,128)S(1)}, u32[]{:S(2)}, u32[]{:S(2)}) collective-permute-start(f32[96,1,128]{2,1,0:T(1,128)S(1)} %get-tuple-element.8), channel_id=1, source_target_pairs={{0,1},{1,2},{2,3},{3,4},{4,5},{5,6},{6,7},{7,8},{8,9},{9,10},{10,1... | collective-permute-start | bytes 147464 | tf_op jit(solution)/shard_map/ppermute | solution.py:17
  32.5 3.1 collective-permute-start.4
  36.9 6.4 %collective-permute-start.7 = (f32[96,1,128]{2,1,0:T(1,128)S(1)}, f32[96,1,128]{2,1,0:T(1,128)S(1)}, u32[]{:S(2)}, u32[]{:S(2)}) collective-permute-start(f32[96,1,128]{2,1,0:T(1,128)S(1)} %get-tuple-element.6), channel_id=1, source_target_pairs={{0,1},{1,2},{2,3},{3,4},{4,5},{5,6},{6,7},{7,8},{8,9},{9,10},{10,1... | collective-permute-start | bytes 147464 | tf_op jit(solution)/shard_map/ppermute | solution.py:17
  42.0 5.1 %copy-start.3 = (s32[256]{0:T(256)S(1)}, s32[256]{0:T(256)}, u32[]{:S(2)}) copy-start(s32[256]{0:T(256)} %param.8) | copy-start | bytes 3076
  42.0 3.1 collective-permute-start.6
  47.1 225.3 %reduce-scatter.3.cloned.1.call-start = ((), (), s32[]{:S(2)}) async-start(), calls=%async_computation.3 | async-start | bytes 6684672 | tf_op jit(solution)/shard_map/reduce_scatter | solution.py:64
  189.9 129.8 %all-gather.5.cloned.1.call-start = ((), (), s32[]{:S(2)}) async-start(), calls=%async_computation.4 | async-start | bytes 3342336 | tf_op jit(solution)/shard_map/all_gather | solution.py:76
  274.1 219.9 %reduce-scatter.5.cloned.1.call-start = ((), (), s32[]{:S(2)}) async-start(), calls=%async_computation.5 | async-start | bytes 6684672 | tf_op jit(solution)/shard_map/reduce_scatter | solution.py:82
  404.0 7.5 %copy-start.2 = (f32[256,96]{0,1:T(8,128)}, f32[256,96]{0,1:T(8,128)S(1)}, u32[]{:S(2)}) copy-start(f32[256,96]{0,1:T(8,128)S(1)} %convolution_bitcast_fusion.2) | copy-start | bytes 294916
Sparse Core Ops, SparseCore 0:
  47.2 50.3 all-gather.2
  190.0 82.2 reduce-scatter.2
  275.1 44.5 all-gather.4
  411.7 82.2 reduce-scatter.4
where the time goes:
time: 503 us; the launch traced here: 502 us
  waiting for transfers between devices  270 us (54%)
  blocking collectives  118 us (23%)
  other arithmetic  44.9 us (9%)
  matrix products  31.1 us (6%)
  starting transfers between devices  22.5 us (4%)
  between operations  14.1 us (3%)
    psum x2, blocking collectives, orthonormalize(): gram_matrix = lax.psum(local_gram, 'row') / total_rows  118 us
    reduce_scatter x1, waiting for transfers between devices, local(): lax.psum_scatter(lax.dot_general(columns, weighted_one, (((0,), (0,)), ((...  82.4 us
    reduce_scatter x1, waiting for transfers between devices, local(): lax.psum_scatter(lax.dot_general(columns, weighted_two, (((0,), (0,)), ((...  82.4 us
    all_gather x1, waiting for transfers between devices, local(): portion = lax.all_gather(omega, 'row', axis=1, tiled=True)  50.3 us
    all_gather x1, waiting for transfers between devices, local(): lax.all_gather(back_local, 'row', axis=0, tiled=True)  45.6 us
    another operation x6, other arithmetic, orthonormalize(): factor = jnp.linalg.cholesky(gram_matrix)  18.9 us
    ppermute x4, starting transfers between devices, with_halo(): before = lax.ppermute(last, axis, up)  17.2 us
    another operation x4, other arithmetic, orthonormalize(): lax.linalg.triangular_solve(factor, sketched, left_side=False, lower=True...  16 us
  transfers between devices with their start and end apart: 12, of which 8 were waited for; matrix products, arithmetic and copies ran while one was open for 0% of the time, Pallas kernels for 0%

commit v1 on v0

--- a/solution.py
+++ b/solution.py
@@ -5,6 +5,12 @@
 
 SWEEPS = 4
 smoothing = 0.24
+
+
+def gather_and_add(value, name):
+    blocks = lax.all_gather(value, name, axis=0, tiled=False)
+    total = blocks.sum(axis=0)
+    return total
 
 
 def with_halo(x, sides, width):
@@ -30,7 +36,7 @@
 
 def orthonormalize(sketched, total_rows):
     local_gram = jnp.dot(sketched.T, sketched, precision=lax.Precision.HIGHEST)
-    gram_matrix = lax.psum(local_gram, "row") / total_rows
+    gram_matrix = gather_and_add(local_gram, "row") / total_rows
     factor = jnp.linalg.cholesky(gram_matrix)
     return lax.linalg.triangular_solve(
         factor, sketched, left_side=False, lower=True, transpose_a=True

time: 503 us -> 427 us (0.85)
  blocking collectives: 118 us -> 42.1 us
    psum x2 -> x0, blocking collectives: 118 us -> none  [orthonormalize(): gram_matrix = lax.psum(local_gram, 'row') / total_rows]
    all_gather x0 -> x2, blocking collectives: none -> 42.1 us  [gather_and_add(): blocks = lax.all_gather(value, name, axis=0, tiled=False)]
where the time goes in v1:
time: 427 us
  waiting for transfers between devices  270 us (63%)
  other arithmetic  45 us (11%)
  blocking collectives  42.1 us (10%)
  matrix products  31.1 us (7%)
  starting transfers between devices  22.5 us (5%)
  between operations  14.1 us (3%)
    reduce_scatter x1, waiting for transfers between devices, local(): lax.psum_scatter(lax.dot_general(columns, weighted_one, (((0,), (0,)), ((...  82.4 us
    reduce_scatter x1, waiting for transfers between devices, local(): lax.psum_scatter(lax.dot_general(columns, weighted_two, (((0,), (0,)), ((...  82.4 us
    all_gather x1, waiting for transfers between devices, local(): portion = lax.all_gather(omega, 'row', axis=1, tiled=True)  50.3 us
    all_gather x1, waiting for transfers between devices, local(): lax.all_gather(back_local, 'row', axis=0, tiled=True)  45.7 us
    all_gather x2, blocking collectives, gather_and_add(): blocks = lax.all_gather(value, name, axis=0, tiled=False)  42.1 us
    another operation x6, other arithmetic, orthonormalize(): factor = jnp.linalg.cholesky(gram_matrix)  18.9 us
    ppermute x4, starting transfers between devices, with_halo(): before = lax.ppermute(last, axis, up)  17.2 us
    another operation x4, other arithmetic, orthonormalize(): lax.linalg.triangular_solve(factor, sketched, left_side=False, lower=True...  16 us
  transfers between devices with their start and end apart: 12, of which 8 were waited for; matrix products, arithmetic and copies ran while one was open for 0% of the time, Pallas kernels for 0%

profile of v1, /device:TPU:0, one launch (start us, length us, event | category | flops | bytes accessed | tf_op | source)
XLA Modules:
  0.0 426.8 jit_solution(1737643794299798763)
XLA Ops:
  7.2 0.0 copy-start
  7.2 0.0 all-gather.5.cloned.1.call-start
  7.2 1.2 fusion.43
  8.5 2.4 collective-permute-start.1
  10.9 1.3 collective-permute-start
  12.2 3.9 collective-permute-done
  16.1 1.9 select_maximum_fusion.6
  18.0 0.3 fusion.24
  18.3 0.1 fusion.42
  18.4 4.7 %collective-permute-start.3 = (f32[96,1,128]{2,1,0:T(1,128)S(1)}, f32[96,1,128]{2,1,0:T(1,128)S(1)}, u32[]{:S(2)}, u32[]{:S(2)}) collective-permute-start(f32[96,1,128]{2,1,0:T(1,128)S(1)} %get-tuple-element.12), channel_id=1, source_target_pairs={{0,1},{1,2},{2,3},{3,4},{4,5},{5,6},{6,7},{7,8},{8,9},{9,10},{10,1... | collective-permute-start | bytes 147464 | tf_op jit(solution)/shard_map/ppermute | solution.py:23
  23.1 1.3 collective-permute-start.2
  24.4 1.8 collective-permute-done.2
  26.2 0.9 select_maximum_fusion.4
  27.1 0.3 fusion.20
  27.4 0.1 fusion.41
  27.5 5.0 %collective-permute-start.5 = (f32[96,1,128]{2,1,0:T(1,128)S(1)}, f32[96,1,128]{2,1,0:T(1,128)S(1)}, u32[]{:S(2)}, u32[]{:S(2)}) collective-permute-start(f32[96,1,128]{2,1,0:T(1,128)S(1)} %get-tuple-element.10), channel_id=1, source_target_pairs={{0,1},{1,2},{2,3},{3,4},{4,5},{5,6},{6,7},{7,8},{8,9},{9,10},{10,1... | collective-permute-start | bytes 147464 | tf_op jit(solution)/shard_map/ppermute | solution.py:23
  32.5 1.3 collective-permute-start.4
  33.8 1.8 collective-permute-done.4
  35.6 0.9 select_maximum_fusion.2
  36.5 0.3 fusion.16
  36.8 0.1 fusion.40
  36.9 5.1 %collective-permute-start.7 = (f32[96,1,128]{2,1,0:T(1,128)S(1)}, f32[96,1,128]{2,1,0:T(1,128)S(1)}, u32[]{:S(2)}, u32[]{:S(2)}) collective-permute-start(f32[96,1,128]{2,1,0:T(1,128)S(1)} %get-tuple-element.8), channel_id=1, source_target_pairs={{0,1},{1,2},{2,3},{3,4},{4,5},{5,6},{6,7},{7,8},{8,9},{9,10},{10,1... | collective-permute-start | bytes 147464 | tf_op jit(solution)/shard_map/ppermute | solution.py:23
  42.0 1.3 collective-permute-start.6
  43.3 1.8 collective-permute-done.6
  45.2 0.9 select_maximum_fusion
  46.1 1.0 fusion.12
  47.1 0.0 all-gather.5.cloned.1.call-update
  47.1 0.0 reduce-scatter.3.cloned.1.call-start
  47.2 0.2 fusion.26
  47.3 50.3 %all-gather.5.cloned.1.call-done = bf16[96,128,128]{2,1,0:T(8,128)(2,1)} async-done(((bf16[96,8,128]{2,1,0:T(8,128)(2,1)}), bf16[96,128,128]{2,1,0:T(8,128)(2,1)}) %all-gather.5.cloned.1.call-update) | async-done | bytes 3145744 | tf_op jit(solution)/shard_map/all_gather | solution.py:59
  97.6 7.7 %fusion.5 = f32[96,256]{1,0:T(8,128)S(1)} fusion(bf16[256,16384]{1,0:T(8,128)(2,1)} %param.7, bf16[12,8,128,128]{3,2,1,0:T(8,128)(2,1)} %bitcast.65, f32[256]{0:T(256)S(1)} %bitcast.66), kind=kOutput, calls=%fused_computation.20 | convolution fusion | flops 805330944 | bytes 11633664 | tf_op jit(solution)/shard_map/dot_general | solution.py:64
  105.4 0.2 fusion.44
  105.6 20.9 %all-gather = f32[1536,96]{1,0:T(8,128)S(1)} all-gather(f32[96,96]{1,0:T(8,128)S(1)} %fusion.44), channel_id=2, replica_groups=mesh['grp'=2,'row'=16] {'row'}, dimensions={0}, use_global_device_ids=true | all-gather | bytes 626688 | tf_op jit(solution)/shard_map/all_gather | solution.py:11
  126.5 0.1 reduce_sum.18
  126.5 0.1 copy.9
  126.6 0.1 copy.10
  126.7 8.8 %cholesky.44 = f32[96,96]{1,0:T(8,128)S(1)} custom-call(f32[96,96]{1,0:T(8,128)S(1)} %fusion.35), custom_call_target="Cholesky" | custom-call | tf_op jit(solution)/shard_map/jit(cholesky)/cholesky | solution.py:40
  135.6 0.6 compare_reduce_fusion.1
  136.2 0.7 fusion.30
  136.9 7.4 %custom-call.6 = f32[1,96,96]{1,2,0:T(8,128)S(1)} custom-call(f32[1,96,96]{2,1,0:T(8,128)S(1)} %fusion.30), custom_call_target="InvertDiagBlocksLowerTriangular" | custom-call | tf_op jit(solution)/shard_map/triangular_solve/custom-call.0 | solution.py:41
  144.2 0.3 fusion.8
  144.5 7.5 %convolution_bitcast_fusion.1 = f32[16384,96]{0,1:T(8,128)} fusion(bf16[256,96]{0,1:T(8,128)(2,1)S(1)} %fusion.8, bf16[256,16384]{1,0:T(8,128)(2,1)} %param.7), kind=kOutput, calls=%fused_computation.1 | convolution fusion | flops 805306368 | bytes 14729216 | tf_op jit(solution)/shard_map/dot_general | solution.py:71
  152.0 0.0 reduce-scatter.3.cloned.1.call-update
  152.0 0.0 all-gather.7.cloned.1.call-start
  152.1 82.4 %reduce-scatter.3.cloned.1.call-done = f32[1024,96]{0,1:T(8,128)} async-done(((f32[16384,96]{0,1:T(8,128)}), f32[1024,96]{0,1:T(8,128)}) %reduce-scatter.3.cloned.1.call-update) | async-done | bytes 393232 | tf_op jit(solution)/shard_map/reduce_scatter | solution.py:70
  234.5 1.7 multiply_convert_fusion
  236.2 0.0 all-gather.7.cloned.1.call-update
  236.2 0.0 reduce-scatter.5.cloned.1.call-start
  236.3 45.7 %all-gather.7.cloned.1.call-done = bf16[16384,96]{0,1:T(8,128)(2,1)} async-done(((bf16[1024,96]{0,1:T(8,128)(2,1)}), bf16[16384,96]{0,1:T(8,128)(2,1)}) %all-gather.7.cloned.1.call-update) | async-done | bytes 3145744 | tf_op jit(solution)/shard_map/all_gather | solution.py:82
  281.9 7.0 %convolution_multiply_fusion = f32[96,256]{1,0:T(8,128)S(1)} fusion(bf16[16384,96]{0,1:T(8,128)(2,1)} %all-gather.7.cloned.1.call-done, bf16[256,16384]{1,0:T(8,128)(2,1)} %param.7, f32[256]{0:T(256)S(1)} %bitcast.68), kind=kOutput, calls=%fused_computation.17 | convolution fusion | flops 805330944 | bytes 11633664 | tf_op jit(solution)/shard_map/dot_general | solution.py:80
  289.0 0.2 fusion.45
  289.2 21.2 %all-gather.1 = f32[1536,96]{1,0:T(8,128)S(1)} all-gather(f32[96,96]{1,0:T(8,128)S(1)} %fusion.45), channel_id=3, replica_groups=mesh['grp'=2,'row'=16] {'row'}, dimensions={0}, use_global_device_ids=true | all-gather | bytes 626688 | tf_op jit(solution)/shard_map/all_gather | solution.py:11
  310.5 0.1 reduce_sum.19
  310.5 0.1 copy.11
  310.7 0.1 copy.12
  310.8 8.8 %cholesky.55 = f32[96,96]{1,0:T(8,128)S(1)} custom-call(f32[96,96]{1,0:T(8,128)S(1)} %fusion.33), custom_call_target="Cholesky" | custom-call | tf_op jit(solution)/shard_map/jit(cholesky)/cholesky | solution.py:40
  319.6 0.6 compare_reduce_fusion
  320.2 0.7 fusion.31
  320.9 7.4 %custom-call.7 = f32[1,96,96]{1,2,0:T(8,128)S(1)} custom-call(f32[1,96,96]{2,1,0:T(8,128)S(1)} %fusion.31), custom_call_target="InvertDiagBlocksLowerTriangular" | custom-call | tf_op jit(solution)/shard_map/triangular_solve/custom-call.0 | solution.py:41
  328.2 0.3 convolution_bitcast_fusion.2
  328.5 7.5 %convolution_bitcast_fusion = f32[16384,96]{0,1:T(8,128)} fusion(bf16[256,16384]{1,0:T(8,128)(2,1)} %param.7, f32[256,96]{0,1:T(8,128)S(1)} %convolution_bitcast_fusion.2, f32[256]{0:T(256)S(1)} %bitcast.69), kind=kOutput, calls=%fused_computation | convolution fusion | flops 805355520 | bytes 14779392 | tf_op jit(solution)/shard_map/dot_general | solution.py:89
  336.1 0.0 reduce-scatter.5.cloned.1.call-update
  336.1 82.4 %reduce-scatter.5.cloned.1.call-done = f32[1024,96]{0,1:T(8,128)} async-done(((f32[16384,96]{0,1:T(8,128)}), f32[1024,96]{0,1:T(8,128)}) %reduce-scatter.5.cloned.1.call-update) | async-done | bytes 393232 | tf_op jit(solution)/shard_map/reduce_scatter | solution.py:88
  418.5 1.8 copy_bitcast_fusion
  (17 shorter events, 0.1 us)
Async XLA Ops:
  7.2 40.0 %copy-start = (f32[8]{0:T(128)S(1)}, f32[8]{0:T(128)}, u32[]{:S(2)}) copy-start(f32[8]{0:T(128)} %param.9) | copy-start | bytes 100
  7.2 10.8 %copy-start.1 = (f32[96,8,128]{2,1,0:T(8,128)S(1)}, f32[96,8,128]{2,1,0:T(8,128)}, u32[]{:S(2)}) copy-start(f32[96,8,128]{2,1,0:T(8,128)} %param.10) | copy-start | bytes 1179652
  7.2 90.5 %all-gather.5.cloned.1.call-start = ((), (), s32[]{:S(2)}) async-start(), calls=%async_computation.2 | async-start | bytes 3342336 | tf_op jit(solution)/shard_map/all_gather | solution.py:59
  8.5 3.7 collective-permute-start.1
  10.9 5.2 %collective-permute-start = (f32[96,1,128]{2,1,0:T(1,128)S(1)}, f32[96,1,128]{2,1,0:T(1,128)S(1)}, u32[]{:S(2)}, u32[]{:S(2)}) collective-permute-start(f32[96,1,128]{2,1,0:T(1,128)S(1)} %get-tuple-element.15), channel_id=1, source_target_pairs={{1,0},{2,1},{3,2},{4,3},{5,4},{6,5},{7,6},{8,7},{9,8},{10,9},{11,1... | collective-permute-start | bytes 147464 | tf_op jit(solution)/shard_map/ppermute | solution.py:24
  18.4 6.0 %collective-permute-start.3 = (f32[96,1,128]{2,1,0:T(1,128)S(1)}, f32[96,1,128]{2,1,0:T(1,128)S(1)}, u32[]{:S(2)}, u32[]{:S(2)}) collective-permute-start(f32[96,1,128]{2,1,0:T(1,128)S(1)} %get-tuple-element.12), channel_id=1, source_target_pairs={{0,1},{1,2},{2,3},{3,4},{4,5},{5,6},{6,7},{7,8},{8,9},{9,10},{10,1... | collective-permute-start | bytes 147464 | tf_op jit(solution)/shard_map/ppermute | solution.py:23
  23.1 3.1 collective-permute-start.2
  27.5 6.3 %collective-permute-start.5 = (f32[96,1,128]{2,1,0:T(1,128)S(1)}, f32[96,1,128]{2,1,0:T(1,128)S(1)}, u32[]{:S(2)}, u32[]{:S(2)}) collective-permute-start(f32[96,1,128]{2,1,0:T(1,128)S(1)} %get-tuple-element.10), channel_id=1, source_target_pairs={{0,1},{1,2},{2,3},{3,4},{4,5},{5,6},{6,7},{7,8},{8,9},{9,10},{10,1... | collective-permute-start | bytes 147464 | tf_op jit(solution)/shard_map/ppermute | solution.py:23
  32.5 3.1 collective-permute-start.4
  36.9 6.4 %collective-permute-start.7 = (f32[96,1,128]{2,1,0:T(1,128)S(1)}, f32[96,1,128]{2,1,0:T(1,128)S(1)}, u32[]{:S(2)}, u32[]{:S(2)}) collective-permute-start(f32[96,1,128]{2,1,0:T(1,128)S(1)} %get-tuple-element.8), channel_id=1, source_target_pairs={{0,1},{1,2},{2,3},{3,4},{4,5},{5,6},{6,7},{7,8},{8,9},{9,10},{10,1... | collective-permute-start | bytes 147464 | tf_op jit(solution)/shard_map/ppermute | solution.py:23
  42.0 5.1 %copy-start.3 = (s32[256]{0:T(256)S(1)}, s32[256]{0:T(256)}, u32[]{:S(2)}) copy-start(s32[256]{0:T(256)} %param.8) | copy-start | bytes 3076
  42.0 3.1 collective-permute-start.6
  47.1 187.4 %reduce-scatter.3.cloned.1.call-start = ((), (), s32[]{:S(2)}) async-start(), calls=%async_computation.3 | async-start | bytes 6684672 | tf_op jit(solution)/shard_map/reduce_scatter | solution.py:70
  152.0 129.9 %all-gather.7.cloned.1.call-start = ((), (), s32[]{:S(2)}) async-start(), calls=%async_computation.4 | async-start | bytes 3342336 | tf_op jit(solution)/shard_map/all_gather | solution.py:82
  236.2 182.3 %reduce-scatter.5.cloned.1.call-start = ((), (), s32[]{:S(2)}) async-start(), calls=%async_computation.5 | async-start | bytes 6684672 | tf_op jit(solution)/shard_map/reduce_scatter | solution.py:88
  328.5 7.5 %copy-start.2 = (f32[256,96]{0,1:T(8,128)}, f32[256,96]{0,1:T(8,128)S(1)}, u32[]{:S(2)}) copy-start(f32[256,96]{0,1:T(8,128)S(1)} %convolution_bitcast_fusion.2) | copy-start | bytes 294916
Sparse Core Ops, SparseCore 0:
  47.2 50.3 all-gather.4
  152.2 82.3 reduce-scatter.2
  237.3 44.6 all-gather.6
  336.2 82.2 reduce-scatter.4
